TPU v7x, 32 devices: a whole 2x2x4 slice. The times are simulated.
32 devices in a mesh: space: 16 (over z, y, core), chan: 2 (over x).
Axes of the slice: x: 2, y: 2, z: 4, core: 2. Of those that a mesh axis runs over, the one named last changes fastest.
Arguments:
- volume: bfloat16 [8, 32, 128, 256], P(None, 'space', None, 'chan'), may hold values from -6 to 6
- first_filter: bfloat16 [3, 3, 3, 256, 256], P(None, None, None, None, 'chan'), may hold values from -0.078125 to 0.078125
- second_filter: bfloat16 [3, 3, 3, 256, 256], P(None, None, None, None, 'chan'), may hold values from -0.078125 to 0.078125
Outputs:
- block_out: bfloat16 [8, 32, 128, 256], P(None, 'space', None, 'chan')
All inputs are finite; a program needn't handle non-finite values.
Results may differ from a plain program's by a relative error of at most 0.0032.
Values may be sent and summed in bfloat16 or wider, within the bound.
A program may use at most 128 MiB of HBM per device.

v0:
```python
import jax
import jax.numpy as jnp
from jax import lax
from jax.sharding import PartitionSpec as P


def padded_2(array, sides, width):
    for axis, dim in sides:
        size, length = (lax.axis_size(axis), array.shape[dim])
        up = [(i, (i + 1) % size) for i in range(size - 1)]
        down = [(j, i) for i, j in up]
        last = lax.slice_in_dim(array, length - width, length, axis=dim)
        first = lax.slice_in_dim(array, 0, width, axis=dim)
        before = lax.ppermute(last, axis, up)
        after = lax.ppermute(first, axis, down)
        array = jnp.concatenate([before, array, after], axis=dim)
    return array


def shifted_sum(padded, weight):
    depth_pad = 1
    padded = jnp.pad(padded, ((depth_pad, depth_pad), (0, 0), (1, 1), (0, 0)))
    depth = padded.shape[0] - 2
    planes = padded.shape[1] - 2
    across = padded.shape[2] - 2
    inputs = padded.shape[3]
    total = jnp.zeros((depth * planes * across, weight.shape[4]), jnp.float32)
    for off_d in range(3):
        for off_h in range(3):
            for off_w in range(3):
                piece = padded[
                    off_d : off_d + depth, off_h : off_h + planes, off_w : off_w + across, :
                ]
                total = total + jnp.dot(
                    piece.reshape(-1, inputs),
                    weight[off_d, off_h, off_w],
                    preferred_element_type=jnp.float32,
                )
    return total.reshape(depth, planes, across, weight.shape[4])


def padded_input(field):
    whole = lax.all_gather(field, "chan", axis=3, tiled=True)
    return padded_2(whole, (("space", 1),), 1)


def per_device(volume, first_filter, second_filter):
    hidden = jnp.maximum(shifted_sum(padded_input(volume), first_filter), 0.0).astype(jnp.bfloat16)
    second = shifted_sum(padded_input(hidden), second_filter)
    total = volume.astype(jnp.float32) + second
    return jnp.maximum(total, 0.0).astype(jnp.bfloat16)


def solution(mesh):
    return jax.shard_map(
        per_device,
        mesh=mesh,
        in_specs=(
            P(None, "space", None, "chan"),
            P(None, None, None, None, "chan"),
            P(None, None, None, None, "chan"),
        ),
        out_specs=P(None, "space", None, "chan"),
        check_vma=False,
    )
```

profile of v0, /device:TPU:1, one launch (start us, length us, event | category | flops | bytes accessed | tf_op | source)
XLA Modules:
  0.0 156.3 jit_solution(18241179619343806776)
XLA Ops:
  7.3 25.0 %all-gather.3.cloned.1.call-done = bf16[8,2,128,256]{3,2,1,0:T(8,128)(2,1)} async-done(((bf16[8,2,128,128]{3,2,1,0:T(8,128)(2,1)}), bf16[8,2,128,256]{3,2,1,0:T(8,128)(2,1)}) %all-gather.3.cloned.1.call-update) | async-done | bytes 1048592 | tf_op jit(solution)/shard_map/all_gather | solution.py:43
  32.3 1.4 fusion.224
  33.6 2.6 %collective-permute-start.1 = (bf16[8,1,128,256]{3,2,1,0:T(8,128)(2,1)S(1)}, bf16[8,1,128,256]{3,2,1,0:T(8,128)(2,1)S(1)}, u32[]{:S(2)}, u32[]{:S(2)}) collective-permute-start(bf16[8,1,128,256]{3,2,1,0:T(8,128)(2,1)S(1)} %get-tuple-element.60), channel_id=1, source_target_pairs={{2,0},{4,2},{6,4},{8,6},{10,8},{12,10},{14,12},{16,14},{18,16},{20... | collective-permute-start | bytes 1572872 | tf_op jit(solution)/shard_map/ppermute | solution.py:15
  36.2 3.0 %collective-permute-start = (bf16[8,1,128,256]{3,2,1,0:T(8,128)(2,1)S(1)}, bf16[8,1,128,256]{3,2,1,0:T(8,128)(2,1)S(1)}, u32[]{:S(2)}, u32[]{:S(2)}) collective-permute-start(bf16[8,1,128,256]{3,2,1,0:T(8,128)(2,1)S(1)} %get-tuple-element.59), channel_id=1, source_target_pairs={{0,2},{2,4},{4,6},{6,8},{8,10},{10,12},{12,14},{14,16},{16,18},{18... | collective-permute-start | bytes 1572872 | tf_op jit(solution)/shard_map/ppermute | solution.py:14
  39.2 2.3 %fusion.138 = f32[2048,128]{1,0:T(8,128)} fusion(bf16[2048,256]{1,0:T(8,128)(2,1)S(1)} %bitcast.272, bf16[3,3,3,256,128]{4,3,2,1,0:T(8,128)(2,1)} %param.4), kind=kOutput, calls=%fused_computation.153 | convolution fusion | flops 134217728 | bytes 2162688 | tf_op jit(solution)/shard_map/dot_general | solution.py:34
  41.6 2.6 %collective-permute-done.1 = bf16[8,1,128,256]{3,2,1,0:T(8,128)(2,1)S(1)} collective-permute-done((bf16[8,1,128,256]{3,2,1,0:T(8,128)(2,1)S(1)}, bf16[8,1,128,256]{3,2,1,0:T(8,128)(2,1)S(1)}, u32[]{:S(2)}, u32[]{:S(2)}) %collective-permute-start.1) | collective-permute-done | bytes 524320 | tf_op jit(solution)/shard_map/ppermute | solution.py:15
  44.2 5.8 %collective-permute-done = bf16[8,1,128,256]{3,2,1,0:T(8,128)(2,1)S(1)} collective-permute-done((bf16[8,1,128,256]{3,2,1,0:T(8,128)(2,1)S(1)}, bf16[8,1,128,256]{3,2,1,0:T(8,128)(2,1)S(1)}, u32[]{:S(2)}, u32[]{:S(2)}) %collective-permute-start) | collective-permute-done | bytes 524320 | tf_op jit(solution)/shard_map/ppermute | solution.py:14
  51.7 2.7 %fusion.222 = (bf16[8,2,128,256]{3,2,1,0:T(8,128)(2,1)}, bf16[8,2,128,256]{3,2,1,0:T(8,128)(2,1)S(1)}, bf16[8,2,128,256]{3,2,1,0:T(8,128)(2,1)S(1)}, bf16[8,2,12...) fusion(bf16[10,4,130,256]{3,2,1,0:T(8,128)(2,1)S(1)} %fusion.10), kind=kLoop, calls=%fused_computation.237 | loop fusion | bytes 10485760 | tf_op jit(solution)/shard_map/slice | solution.py:31
  54.4 6.7 %fusion.221 = (bf16[8,2,128,256]{3,2,1,0:T(8,128)(2,1)}, bf16[8,2,128,256]{3,2,1,0:T(8,128)(2,1)}, bf16[8,2,128,256]{3,2,1,0:T(8,128)(2,1)}, bf16[8,2,128,256]{3...) fusion(bf16[10,4,130,256]{3,2,1,0:T(8,128)(2,1)S(1)} %fusion.10), kind=kLoop, calls=%fused_computation.236 | loop fusion | bytes 39845888 | tf_op jit(solution)/shard_map/slice | solution.py:31
  61.2 1.8 %fusion.113 = f32[2048,128]{1,0:T(8,128)S(1)} fusion(bf16[2048,256]{1,0:T(8,128)(2,1)} %bitcast.306, bf16[3,3,3,256,128]{4,3,2,1,0:T(8,128)(2,1)} %param.4), kind=kOutput, calls=%fused_computation.128 | convolution fusion | flops 134217728 | bytes 2162688 | tf_op jit(solution)/shard_map/dot_general | solution.py:34
  63.0 1.4 fusion.115
  78.5 1.6 %fusion.60 = bf16[2048,128]{1,0:T(8,128)(2,1)} fusion(f32[2048,128]{1,0:T(8,128)S(1)} %fusion.113, f32[2048,128]{1,0:T(8,128)S(1)} %fusion.115, f32[2048,128]{1,0:T(8,128)S(1)} %fusion.117, f32[2048,128]{1,0:T(8,128)S(1)} %fusion.119, f32[2048,128]{1,0:T(8,128)S(1)} %fusion.121, f32[2048,128]{1,0:T(8,128)S(1)} %fusion.123, f32[2048,128]{1,0:T(8,128)S(1)} %fusion.125, ...), kind=kOutput, calls=%fused_computation.70 | convolution fusion | flops 138149888 | bytes 15269888 | tf_op jit(solution)/shard_map/dot_general | solution.py:34
  80.1 21.2 %all-gather.5.cloned.1.call-done = bf16[8,2,128,256]{3,2,1,0:T(8,128)(2,1)} async-done(((bf16[8,2,128,128]{3,2,1,0:T(8,128)(2,1)}), bf16[8,2,128,256]{3,2,1,0:T(8,128)(2,1)}) %all-gather.5.cloned.1.call-update) | async-done | bytes 1048592 | tf_op jit(solution)/shard_map/all_gather | solution.py:43
  101.3 1.4 fusion.223
  102.7 2.6 %collective-permute-start.3 = (bf16[8,1,128,256]{3,2,1,0:T(8,128)(2,1)S(1)}, bf16[8,1,128,256]{3,2,1,0:T(8,128)(2,1)S(1)}, u32[]{:S(2)}, u32[]{:S(2)}) collective-permute-start(bf16[8,1,128,256]{3,2,1,0:T(8,128)(2,1)S(1)} %get-tuple-element.56), channel_id=1, source_target_pairs={{2,0},{4,2},{6,4},{8,6},{10,8},{12,10},{14,12},{16,14},{18,16},{20... | collective-permute-start | bytes 1572872 | tf_op jit(solution)/shard_map/ppermute | solution.py:15
  105.3 3.0 %collective-permute-start.2 = (bf16[8,1,128,256]{3,2,1,0:T(8,128)(2,1)S(1)}, bf16[8,1,128,256]{3,2,1,0:T(8,128)(2,1)S(1)}, u32[]{:S(2)}, u32[]{:S(2)}) collective-permute-start(bf16[8,1,128,256]{3,2,1,0:T(8,128)(2,1)S(1)} %get-tuple-element.55), channel_id=1, source_target_pairs={{0,2},{2,4},{4,6},{6,8},{8,10},{10,12},{12,14},{14,16},{16,18},{18... | collective-permute-start | bytes 1572872 | tf_op jit(solution)/shard_map/ppermute | solution.py:14
  108.3 2.3 %fusion.86 = f32[2048,128]{1,0:T(8,128)} fusion(bf16[2048,256]{1,0:T(8,128)(2,1)S(1)} %bitcast.273, bf16[3,3,3,256,128]{4,3,2,1,0:T(8,128)(2,1)} %param.5), kind=kOutput, calls=%fused_computation.101 | convolution fusion | flops 134217728 | bytes 2162688 | tf_op jit(solution)/shard_map/dot_general | solution.py:34
  110.6 2.6 %collective-permute-done.3 = bf16[8,1,128,256]{3,2,1,0:T(8,128)(2,1)S(1)} collective-permute-done((bf16[8,1,128,256]{3,2,1,0:T(8,128)(2,1)S(1)}, bf16[8,1,128,256]{3,2,1,0:T(8,128)(2,1)S(1)}, u32[]{:S(2)}, u32[]{:S(2)}) %collective-permute-start.3) | collective-permute-done | bytes 524320 | tf_op jit(solution)/shard_map/ppermute | solution.py:15
  113.2 5.8 %collective-permute-done.2 = bf16[8,1,128,256]{3,2,1,0:T(8,128)(2,1)S(1)} collective-permute-done((bf16[8,1,128,256]{3,2,1,0:T(8,128)(2,1)S(1)}, bf16[8,1,128,256]{3,2,1,0:T(8,128)(2,1)S(1)}, u32[]{:S(2)}, u32[]{:S(2)}) %collective-permute-start.2) | collective-permute-done | bytes 524320 | tf_op jit(solution)/shard_map/ppermute | solution.py:14
  119.8 1.0 select_maximum_fusion
  120.7 2.7 %fusion.220 = (bf16[8,2,128,256]{3,2,1,0:T(8,128)(2,1)}, bf16[8,2,128,256]{3,2,1,0:T(8,128)(2,1)S(1)}, bf16[8,2,128,256]{3,2,1,0:T(8,128)(2,1)S(1)}, bf16[8,2,12...) fusion(bf16[10,4,130,256]{3,2,1,0:T(8,128)(2,1)S(1)} %select_maximum_fusion), kind=kLoop, calls=%fused_computation.235 | loop fusion | bytes 10485760 | tf_op jit(solution)/shard_map/slice | solution.py:31
  123.4 6.7 %fusion.219 = (bf16[8,2,128,256]{3,2,1,0:T(8,128)(2,1)}, bf16[8,2,128,256]{3,2,1,0:T(8,128)(2,1)}, bf16[8,2,128,256]{3,2,1,0:T(8,128)(2,1)}, bf16[8,2,128,256]{3...) fusion(bf16[10,4,130,256]{3,2,1,0:T(8,128)(2,1)S(1)} %select_ma, ...), kind=kLoop, calls=%fused_computation.234 | loop fusion | bytes 39845888 | tf_op jit(solution)/shard_map/slice | solution.py:31
  130.2 1.8 %fusion.61 = f32[2048,128]{1,0:T(8,128)S(1)} fusion(bf16[2048,256]{1,0:T(8,128)(2,1)} %bitcast.308, bf16[3,3,3,256,128]{4,3,2,1,0:T(8,128)(2,1)} %param.5), kind=kOutput, calls=%fused_computation.76 | convolution fusion | flops 134217728 | bytes 2162688 | tf_op jit(solution)/shard_map/dot_general | solution.py:34
  132.0 1.3 fusion.63
  (137 shorter events, 33.0 us)
Async XLA Ops:
  6.5 25.7 %all-gather.3.cloned.1.call-start = ((), (), s32[]{:S(2)}) async-start(), calls=%async_computation | async-start | bytes 1572864 | tf_op jit(solution)/shard_map/all_gather | solution.py:43
  7.3 94.0 %all-gather.5.cloned.1.call-start = ((), (), s32[]{:S(2)}) async-start(), calls=%async_computation.1 | async-start | bytes 1572864 | tf_op jit(solution)/shard_map/all_gather | solution.py:43
  32.3 7.0 %copy-start = (bf16[8,2,128,256]{3,2,1,0:T(8,128)(2,1)S(1)}, bf16[8,2,128,256]{3,2,1,0:T(8,128)(2,1)}, u32[]{:S(2)}) copy-start(bf16[8,2,128,256]{3,2,1,0:T(8,128)(2,1)} %all-gather.3.cloned.1.call-done) | copy-start | bytes 3145732
  33.6 10.5 %collective-permute-start.1 = (bf16[8,1,128,256]{3,2,1,0:T(8,128)(2,1)S(1)}, bf16[8,1,128,256]{3,2,1,0:T(8,128)(2,1)S(1)}, u32[]{:S(2)}, u32[]{:S(2)}) collective-permute-start(bf16[8,1,128,256]{3,2,1,0:T(8,128)(2,1)S(1)} %get-tuple-element.60), channel_id=1, source_target_pairs={{2,0},{4,2},{6,4},{8,6},{10,8},{12,10},{14,12},{16,14},{18,16},{20... | collective-permute-start | bytes 1572872 | tf_op jit(solution)/shard_map/ppermute | solution.py:15
  36.2 13.7 %collective-permute-start = (bf16[8,1,128,256]{3,2,1,0:T(8,128)(2,1)S(1)}, bf16[8,1,128,256]{3,2,1,0:T(8,128)(2,1)S(1)}, u32[]{:S(2)}, u32[]{:S(2)}) collective-permute-start(bf16[8,1,128,256]{3,2,1,0:T(8,128)(2,1)S(1)} %get-tuple-element.59), channel_id=1, source_target_pairs={{0,2},{2,4},{4,6},{6,8},{8,10},{10,12},{12,14},{14,16},{16,18},{18... | collective-permute-start | bytes 1572872 | tf_op jit(solution)/shard_map/ppermute | solution.py:14
  44.2 5.8 %copy-start.31 = (bf16[8,1,128,256]{3,2,1,0:T(8,128)(2,1)}, bf16[8,1,128,256]{3,2,1,0:T(8,128)(2,1)S(1)}, u32[]{:S(2)}) copy-start(bf16[8,1,128,256]{3,2,1,0:T(8,128)(2,1)S(1)} %collective-permute-done.1) | copy-start | bytes 1572868
  61.1 1.8 %copy-start.22 = (bf16[8,2,128,256]{3,2,1,0:T(8,128)(2,1)S(1)}, bf16[8,2,128,256]{3,2,1,0:T(8,128)(2,1)}, u32[]{:S(2)}) copy-start(bf16[8,2,128,256]{3,2,1,0:T(8,128)(2,1)} %get-tuple-element.30) | copy-start | bytes 3145732
  61.1 3.2 %copy-start.20 = (bf16[8,2,128,256]{3,2,1,0:T(8,128)(2,1)S(1)}, bf16[8,2,128,256]{3,2,1,0:T(8,128)(2,1)}, u32[]{:S(2)}) copy-start(bf16[8,2,128,256]{3,2,1,0:T(8,128)(2,1)} %get-tuple-element.31) | copy-start | bytes 3145732
  61.2 3.2 %copy-start.39 = (bf16[3,3,3,256,128]{4,3,2,1,0:T(8,128)(2,1)S(1)}, bf16[3,3,3,256,128]{4,3,2,1,0:T(8,128)(2,1)}, u32[]{:S(2)}) copy-start(bf16[3,3,3,256,128]{4,3,2,1,0:T(8,128)(2,1)} %param.4) | copy-start | bytes 5308420
  63.0 1.8 %copy-start.18 = (bf16[8,2,128,256]{3,2,1,0:T(8,128)(2,1)S(1)}, bf16[8,2,128,256]{3,2,1,0:T(8,128)(2,1)}, u32[]{:S(2)}) copy-start(bf16[8,2,128,256]{3,2,1,0:T(8,128)(2,1)} %get-tuple-element.32) | copy-start | bytes 3145732
  64.8 1.3 copy-start.14
  69.7 1.6 %copy-start.2 = (bf16[8,2,128,256]{3,2,1,0:T(8,128)(2,1)S(1)}, bf16[8,2,128,256]{3,2,1,0:T(8,128)(2,1)}, u32[]{:S(2)}) copy-start(bf16[8,2,128,256]{3,2,1,0:T(8,128)(2,1)} %get-tuple-element.40) | copy-start | bytes 3145732
  75.7 1.5 copy-start.28
  101.3 7.0 %copy-start.1 = (bf16[8,2,128,256]{3,2,1,0:T(8,128)(2,1)S(1)}, bf16[8,2,128,256]{3,2,1,0:T(8,128)(2,1)}, u32[]{:S(2)}) copy-start(bf16[8,2,128,256]{3,2,1,0:T(8,128)(2,1)} %all-gather.5.cloned.1.call-done) | copy-start | bytes 3145732
  102.7 10.5 %collective-permute-start.3 = (bf16[8,1,128,256]{3,2,1,0:T(8,128)(2,1)S(1)}, bf16[8,1,128,256]{3,2,1,0:T(8,128)(2,1)S(1)}, u32[]{:S(2)}, u32[]{:S(2)}) collective-permute-start(bf16[8,1,128,256]{3,2,1,0:T(8,128)(2,1)S(1)} %get-tuple-element.56), channel_id=1, source_target_pairs={{2,0},{4,2},{6,4},{8,6},{10,8},{12,10},{14,12},{16,14},{18,16},{20... | collective-permute-start | bytes 1572872 | tf_op jit(solution)/shard_map/ppermute | solution.py:15
  105.3 13.7 %collective-permute-start.2 = (bf16[8,1,128,256]{3,2,1,0:T(8,128)(2,1)S(1)}, bf16[8,1,128,256]{3,2,1,0:T(8,128)(2,1)S(1)}, u32[]{:S(2)}, u32[]{:S(2)}) collective-permute-start(bf16[8,1,128,256]{3,2,1,0:T(8,128)(2,1)S(1)} %get-tuple-element.55), channel_id=1, source_target_pairs={{0,2},{2,4},{4,6},{6,8},{8,10},{10,12},{12,14},{14,16},{16,18},{18... | collective-permute-start | bytes 1572872 | tf_op jit(solution)/shard_map/ppermute | solution.py:14
  113.2 5.8 %copy-start.33 = (bf16[8,1,128,256]{3,2,1,0:T(8,128)(2,1)}, bf16[8,1,128,256]{3,2,1,0:T(8,128)(2,1)S(1)}, u32[]{:S(2)}) copy-start(bf16[8,1,128,256]{3,2,1,0:T(8,128)(2,1)S(1)} %collective-permute-done.3) | copy-start | bytes 1572868
  130.2 1.8 %copy-start.23 = (bf16[8,2,128,256]{3,2,1,0:T(8,128)(2,1)S(1)}, bf16[8,2,128,256]{3,2,1,0:T(8,128)(2,1)}, u32[]{:S(2)}) copy-start(bf16[8,2,128,256]{3,2,1,0:T(8,128)(2,1)} %get-tuple-element.6) | copy-start | bytes 3145732
  130.2 3.2 %copy-start.21 = (bf16[8,2,128,256]{3,2,1,0:T(8,128)(2,1)S(1)}, bf16[8,2,128,256]{3,2,1,0:T(8,128)(2,1)}, u32[]{:S(2)}) copy-start(bf16[8,2,128,256]{3,2,1,0:T(8,128)(2,1)} %get-tuple-element.7) | copy-start | bytes 3145732
  130.2 3.2 %copy-start.40 = (bf16[3,3,3,256,128]{4,3,2,1,0:T(8,128)(2,1)S(1)}, bf16[3,3,3,256,128]{4,3,2,1,0:T(8,128)(2,1)}, u32[]{:S(2)}) copy-start(bf16[3,3,3,256,128]{4,3,2,1,0:T(8,128)(2,1)} %param.5) | copy-start | bytes 5308420
  132.0 1.8 %copy-start.19 = (bf16[8,2,128,256]{3,2,1,0:T(8,128)(2,1)S(1)}, bf16[8,2,128,256]{3,2,1,0:T(8,128)(2,1)}, u32[]{:S(2)}) copy-start(bf16[8,2,128,256]{3,2,1,0:T(8,128)(2,1)} %get-tuple-element.8) | copy-start | bytes 3145732
  133.8 1.3 copy-start.15
  138.7 1.6 %copy-start.3 = (bf16[8,2,128,256]{3,2,1,0:T(8,128)(2,1)S(1)}, bf16[8,2,128,256]{3,2,1,0:T(8,128)(2,1)}, u32[]{:S(2)}) copy-start(bf16[8,2,128,256]{3,2,1,0:T(8,128)(2,1)} %get-tuple-element.16) | copy-start | bytes 3145732
  144.7 1.5 copy-start.29
  (23 other events, 27.7 us)
Sparse Core Ops, SparseCore 0:
  8.9 23.3 all-gather.2
  80.2 21.0 all-gather.4
where the time goes:
time: 157 us; the launch traced here: 156 us
  waiting for transfers between devices  63.7 us (41%)
  matrix products  33.4 us (21%)
  local copies, waits for them, and re-layouts  30.6 us (19%)
  between operations  14.1 us (9%)
  starting transfers between devices  11.2 us (7%)
  other arithmetic  3.25 us (2%)
    all_gather x2, waiting for transfers between devices, padded_input(): whole = lax.all_gather(field, 'chan', axis=3, tiled=True)  46.2 us
    dot_general x54, matrix products, shifted_sum(): jnp.dot(piece.reshape(-1, inputs), weight[off_d, off_h, off_w], preferred...  33.4 us
    slice x4, local copies, waits for them, and re-layouts, shifted_sum(): padded[off_d:off_d + depth, off_h:off_h + planes, off_w:off_w + across, :]  18.8 us
    ppermute x2, waiting for transfers between devices, padded_2(): before = lax.ppermute(last, axis, up)  11.6 us
    unnamed x82, local copies, waits for them, and re-layouts  9.03 us
    ppermute x2, starting transfers between devices, padded_2(): before = lax.ppermute(last, axis, up)  6 us
    ppermute x2, waiting for transfers between devices, padded_2(): after = lax.ppermute(first, axis, down)  5.21 us
    ppermute x2, starting transfers between devices, padded_2(): after = lax.ppermute(first, axis, down)  5.17 us
  transfers between devices with their start and end apart: 6, of which 6 were waited for; matrix products, arithmetic and copies ran while one was open for 3% of the time, Pallas kernels for 0%

commit v1 on v0

v1 whole, which is shorter than its diff:
```python
import functools

import jax
import jax.numpy as jnp
from jax import lax
from jax.experimental import pallas as pl
from jax.experimental.pallas import tpu as pltpu
from jax.sharding import PartitionSpec as P

MESH = pl.DeviceIdType.MESH
CHAN, OWN_UP, OWN_DOWN, FWD_UP, FWD_DOWN = range(5)


def shifted_out(partial, out_c):
    width = partial.shape[0]
    at = lax.broadcasted_iota(jnp.int32, (width, out_c), 0)
    left = pltpu.roll(partial[:, :out_c], 1, 0)
    right = pltpu.roll(partial[:, 2 * out_c :], width - 1, 0)
    left = jnp.where(at == 0, 0.0, left)
    right = jnp.where(at == width - 1, 0.0, right)
    return left + partial[:, out_c : 2 * out_c] + right


def kernel(
    n_space, volume, first, second, out,
    field, hidden, w1, w2, local_sem, send_sem, recv_sem,
):
    s, c = lax.axis_index("space"), lax.axis_index("chan")
    other = 1 - c
    depth, planes, width, half = volume.shape
    out_c = first.shape[4]
    has_up, has_down = s < n_space - 1, s > 0
    up, down, across = {"space": s + 1}, {"space": s - 1}, {"chan": other}

    own_copy = pltpu.make_async_copy(
        volume, field.at[c, pl.ds(1, depth), pl.ds(1, planes)], local_sem.at[0]
    )
    own_copy.start()
    filter_copies = []
    for k, (src, dst) in enumerate(((first, w1), (second, w2))):
        for tap in range(3):
            filter_copies.append(
                pltpu.make_async_copy(
                    src.at[:, :, tap],
                    dst.at[:, :, :, pl.ds(tap * out_c, out_c)],
                    local_sem.at[1 + 3 * k + tap],
                )
            )
    for copy in filter_copies:
        copy.start()

    barrier = pltpu.get_barrier_semaphore()
    pl.semaphore_signal(barrier, inc=1, device_id=across, device_id_type=MESH)

    @pl.when(has_up)
    def _():
        pl.semaphore_signal(barrier, inc=1, device_id=up, device_id_type=MESH)

    @pl.when(has_down)
    def _():
        pl.semaphore_signal(barrier, inc=1, device_id=down, device_id_type=MESH)

    line = jnp.zeros((planes + 2, width, half), field.dtype)
    for buf in (field, hidden):
        for h in range(2):
            buf[h, 0] = line
            buf[h, depth + 1] = line

    @pl.when(jnp.logical_not(has_down))
    def _():
        for buf in (field, hidden):
            for h in range(2):
                buf[h, :, 0] = jnp.zeros((depth + 2, width, half), field.dtype)

    @pl.when(jnp.logical_not(has_up))
    def _():
        for buf in (field, hidden):
            for h in range(2):
                buf[h, :, planes + 1] = jnp.zeros((depth + 2, width, half), field.dtype)

    pl.semaphore_wait(barrier, 1 + has_up.astype(jnp.int32) + has_down.astype(jnp.int32))

    def remote(phase, kind, d, own_src=None):
        buf = field if phase == 0 else hidden
        which = other if kind in (FWD_UP, FWD_DOWN) else c
        if kind == CHAN:
            src, dst, dev = pl.ds(1, planes), pl.ds(1, planes), across
        elif kind in (OWN_UP, FWD_UP):
            src, dst, dev = pl.ds(planes, 1), pl.ds(0, 1), up
        else:
            src, dst, dev = pl.ds(1, 1), pl.ds(planes + 1, 1), down
        source = buf.at[which, d + 1, src]
        return pltpu.make_async_remote_copy(
            src_ref=source,
            dst_ref=buf.at[which, d + 1, dst],
            send_sem=send_sem.at[phase, kind, d],
            recv_sem=recv_sem.at[phase, kind, d],
            device_id=dev,
            device_id_type=MESH,
        )

    def send_own(phase, d):
        remote(phase, CHAN, d).start()

        @pl.when(has_up)
        def _():
            remote(phase, OWN_UP, d).start()

        @pl.when(has_down)
        def _():
            remote(phase, OWN_DOWN, d).start()

    def forward(phase, d):
        remote(phase, CHAN, d).wait_recv()

        @pl.when(has_up)
        def _():
            remote(phase, FWD_UP, d).start()

        @pl.when(has_down)
        def _():
            remote(phase, FWD_DOWN, d).start()

    def await_halo(phase, d):
        @pl.when(has_down)
        def _():
            remote(phase, OWN_UP, d).wait_recv()
            remote(phase, FWD_UP, d).wait_recv()

        @pl.when(has_up)
        def _():
            remote(phase, OWN_DOWN, d).wait_recv()
            remote(phase, FWD_DOWN, d).wait_recv()

    def conv(buf, w, d):
        pieces = [
            buf[h, d + a, b : b + planes].reshape(planes * width, half)
            for a in range(3)
            for b in range(3)
            for h in range(2)
        ]
        lhs = jnp.concatenate(pieces, axis=1)
        partial = jnp.dot(
            lhs, w[...].reshape(lhs.shape[1], 3 * out_c), preferred_element_type=jnp.float32
        )
        return [shifted_out(partial[p * width : (p + 1) * width], out_c) for p in range(planes)]

    own_copy.wait()

    def send_volume(d, carry):
        send_own(0, d)
        return carry

    lax.fori_loop(0, depth, send_volume, 0)
    for copy in filter_copies[:3]:
        copy.wait()

    def conv_phase(phase, finish):
        def step(t, carry):
            @pl.when(t < depth)
            def _():
                forward(phase, t)

            @pl.when(jnp.logical_and(t >= 1, t <= depth))
            def _():
                await_halo(phase, t - 1)

            @pl.when(t >= 2)
            def _():
                finish(t - 2)

            return carry

        lax.fori_loop(0, depth + 2, step, 0)

    def finish_hidden(d):
        for p, total in enumerate(conv(field, w1, d)):
            hidden[c, d + 1, p + 1] = jnp.maximum(total, 0.0).astype(hidden.dtype)
        send_own(1, d)

    def finish_out(d):
        for p, total in enumerate(conv(hidden, w2, d)):
            total = total + field[c, d + 1, p + 1].astype(jnp.float32)
            out[d, p] = jnp.maximum(total, 0.0).astype(out.dtype)

    conv_phase(0, finish_hidden)
    for copy in filter_copies[3:]:
        copy.wait()
    conv_phase(1, finish_out)

    def drain(d, carry):
        for phase in range(2):
            remote(phase, CHAN, d).wait_send()

            @pl.when(has_up)
            def _():
                remote(phase, OWN_UP, d).wait_send()
                remote(phase, FWD_UP, d).wait_send()

            @pl.when(has_down)
            def _():
                remote(phase, OWN_DOWN, d).wait_send()
                remote(phase, FWD_DOWN, d).wait_send()

        return carry

    lax.fori_loop(0, depth, drain, 0)


def per_device(n_space, volume, first_filter, second_filter):
    depth, planes, width, half = volume.shape
    taps_d, taps_h, taps_w, in_c, out_c = first_filter.shape
    plane_buf = pltpu.VMEM((2, depth + 2, planes + 2, width, half), jnp.bfloat16)
    filter_buf = pltpu.VMEM((taps_d, taps_h, in_c, taps_w * out_c), jnp.bfloat16)
    flops = 2 * 2 * 27 * depth * planes * width * in_c * out_c
    return pl.pallas_call(
        functools.partial(kernel, n_space),
        out_shape=jax.ShapeDtypeStruct(volume.shape, jnp.bfloat16),
        in_specs=[pl.BlockSpec(memory_space=pltpu.HBM)] * 3,
        out_specs=pl.BlockSpec(memory_space=pltpu.VMEM),
        scratch_shapes=[
            plane_buf,
            plane_buf,
            filter_buf,
            filter_buf,
            pltpu.SemaphoreType.DMA((7,)),
            pltpu.SemaphoreType.DMA((2, 5, depth)),
            pltpu.SemaphoreType.DMA((2, 5, depth)),
        ],
        compiler_params=pltpu.CompilerParams(
            collective_id=0, has_side_effects=True, vmem_limit_bytes=40 << 20
        ),
        cost_estimate=pl.CostEstimate(
            flops=flops, bytes_accessed=4 * volume.size + 4 * first_filter.size, transcendentals=0
        ),
    )(volume, first_filter, second_filter)


def solution(mesh):
    return jax.shard_map(
        functools.partial(per_device, mesh.shape["space"]),
        mesh=mesh,
        in_specs=(
            P(None, "space", None, "chan"),
            P(None, None, None, None, "chan"),
            P(None, None, None, None, "chan"),
        ),
        out_specs=P(None, "space", None, "chan"),
        check_vma=False,
    )
```

time: 157 us -> 48.7 us (0.31)
  the two profiles are of different devices: /device:TPU:1 before, /device:TPU:19 now
where the time goes in v1:
time: 48.7 us; the launch traced here: 48.5 us
  Pallas kernels  43.7 us (90%)
  local copies, waits for them, and re-layouts  4.79 us (10%)
    pallas_call x1, Pallas kernels, per_device(): pl.pallas_call(functools.partial(kernel, n_space), out_shape=jax.ShapeDty...  43.7 us
    unnamed x7, local copies, waits for them, and re-layouts  4.79 us

profile of v1, /device:TPU:19, one launch (start us, length us, event | category | flops | bytes accessed | tf_op | source)
XLA Modules:
  0.0 48.5 jit_solution(8448879605845289840)
XLA Ops:
  0.0 0.0 copy-start
  0.0 1.5 %copy-done = bf16[3,3,3,256,128]{4,3,2,1,0:T(8,128)(2,1)S(1)} copy-done((bf16[3,3,3,256,128]{4,3,2,1,0:T(8,128)(2,1)S(1)}, bf16[3,3,3,256,128]{4,3,2,1,0:T(8,128)(2,1)}, u32[]{:S(2)}) %copy-start) | copy-done | bytes 1769496
  1.5 0.0 copy-start.1
  1.5 1.5 %copy-done.1 = bf16[3,3,3,256,128]{4,3,2,1,0:T(8,128)(2,1)S(1)} copy-done((bf16[3,3,3,256,128]{4,3,2,1,0:T(8,128)(2,1)S(1)}, bf16[3,3,3,256,128]{4,3,2,1,0:T(8,128)(2,1)}, u32[]{:S(2)}) %copy-start.1) | copy-done | bytes 1769496
  3.0 0.0 copy-start.2
  3.0 1.0 %copy-done.2 = bf16[8,2,128,128]{3,2,1,0:T(8,128)(2,1)S(1)} copy-done((bf16[8,2,128,128]{3,2,1,0:T(8,128)(2,1)S(1)}, bf16[8,2,128,128]{3,2,1,0:T(8,128)(2,1)}, u32[]{:S(2)}) %copy-start.2) | copy-done | bytes 524312
  4.0 43.7 %shard_map.37 = bf16[8,2,128,128]{3,2,1,0:T(8,128)(2,1)S(1)} custom-call(bf16[8,2,128,128]{3,2,1,0:T(8,128)(2,1)S(1)} %copy-done.2, bf16[3,3,3,256,128]{4,3,2,1,0:T(8,128)(2,1)S(1)} %copy-done, bf16[3,3,3,256,128]{4,3,2,1,0:T(8,128)(2,1)S(1)} %copy-done.1), custom_call_target="tpu_custom_call" | custom-call | flops 7247757312 | bytes 4587520 | tf_op jit(solution)/shard_map/pallas_call | solution.py:216
  47.7 0.8 %copy.5 = bf16[8,2,128,128]{3,2,1,0:T(8,128)(2,1)} copy(bf16[8,2,128,128]{3,2,1,0:T(8,128)(2,1)S(1)} %shard_map.37) | data formatting | bytes 1048576
Async XLA Ops:
  0.0 1.5 %copy-start = (bf16[3,3,3,256,128]{4,3,2,1,0:T(8,128)(2,1)S(1)}, bf16[3,3,3,256,128]{4,3,2,1,0:T(8,128)(2,1)}, u32[]{:S(2)}) copy-start(bf16[3,3,3,256,128]{4,3,2,1,0:T(8,128)(2,1)} %first.1) | copy-start | bytes 5308420
  1.5 1.5 %copy-start.1 = (bf16[3,3,3,256,128]{4,3,2,1,0:T(8,128)(2,1)S(1)}, bf16[3,3,3,256,128]{4,3,2,1,0:T(8,128)(2,1)}, u32[]{:S(2)}) copy-start(bf16[3,3,3,256,128]{4,3,2,1,0:T(8,128)(2,1)} %second.1) | copy-start | bytes 5308420
  3.0 1.0 %copy-start.2 = (bf16[8,2,128,128]{3,2,1,0:T(8,128)(2,1)S(1)}, bf16[8,2,128,128]{3,2,1,0:T(8,128)(2,1)}, u32[]{:S(2)}) copy-start(bf16[8,2,128,128]{3,2,1,0:T(8,128)(2,1)} %volume.1) | copy-start | bytes 1572868

commit v2 on v1

--- a/solution.py
+++ b/solution.py
@@ -8,6 +8,7 @@
 from jax.sharding import PartitionSpec as P
 
 MESH = pl.DeviceIdType.MESH
+LEADS = (4, 4)
 CHAN, OWN_UP, OWN_DOWN, FWD_UP, FWD_DOWN = range(5)
 
 
@@ -80,7 +81,7 @@
 
     pl.semaphore_wait(barrier, 1 + has_up.astype(jnp.int32) + has_down.astype(jnp.int32))
 
-    def remote(phase, kind, d, own_src=None):
+    def remote(phase, kind, d):
         buf = field if phase == 0 else hidden
         which = other if kind in (FWD_UP, FWD_DOWN) else c
         if kind == CHAN:
@@ -89,7 +90,14 @@
             src, dst, dev = pl.ds(planes, 1), pl.ds(0, 1), up
         else:
             src, dst, dev = pl.ds(1, 1), pl.ds(planes + 1, 1), down
-        source = buf.at[which, d + 1, src]
+        if phase == 0 and kind == CHAN:
+            source = volume.at[d]
+        elif phase == 0 and kind == OWN_UP:
+            source = volume.at[d, pl.ds(planes - 1, 1)]
+        elif phase == 0 and kind == OWN_DOWN:
+            source = volume.at[d, pl.ds(0, 1)]
+        else:
+            source = buf.at[which, d + 1, src]
         return pltpu.make_async_remote_copy(
             src_ref=source,
             dst_ref=buf.at[which, d + 1, dst],
@@ -145,33 +153,32 @@
         )
         return [shifted_out(partial[p * width : (p + 1) * width], out_c) for p in range(planes)]
 
-    own_copy.wait()
-
     def send_volume(d, carry):
         send_own(0, d)
         return carry
 
     lax.fori_loop(0, depth, send_volume, 0)
+    own_copy.wait()
     for copy in filter_copies[:3]:
         copy.wait()
 
-    def conv_phase(phase, finish):
+    def conv_phase(phase, lead, finish):
         def step(t, carry):
             @pl.when(t < depth)
             def _():
                 forward(phase, t)
 
-            @pl.when(jnp.logical_and(t >= 1, t <= depth))
-            def _():
-                await_halo(phase, t - 1)
-
-            @pl.when(t >= 2)
-            def _():
-                finish(t - 2)
+            @pl.when(jnp.logical_and(t >= lead - 1, t < lead - 1 + depth))
+            def _():
+                await_halo(phase, t - (lead - 1))
+
+            @pl.when(t >= lead)
+            def _():
+                finish(t - lead)
 
             return carry
 
-        lax.fori_loop(0, depth + 2, step, 0)
+        lax.fori_loop(0, depth + lead, step, 0)
 
     def finish_hidden(d):
         for p, total in enumerate(conv(field, w1, d)):
@@ -183,10 +190,10 @@
             total = total + field[c, d + 1, p + 1].astype(jnp.float32)
             out[d, p] = jnp.maximum(total, 0.0).astype(out.dtype)
 
-    conv_phase(0, finish_hidden)
+    conv_phase(0, LEADS[0], finish_hidden)
     for copy in filter_copies[3:]:
         copy.wait()
-    conv_phase(1, finish_out)
+    conv_phase(1, LEADS[1], finish_out)
 
     def drain(d, carry):
         for phase in range(2):
@@ -228,7 +235,7 @@
             pltpu.SemaphoreType.DMA((2, 5, depth)),
         ],
         compiler_params=pltpu.CompilerParams(
-            collective_id=0, has_side_effects=True, vmem_limit_bytes=40 << 20
+            collective_id=0, has_side_effects=True, vmem_limit_bytes=60 << 20
         ),
         cost_estimate=pl.CostEstimate(
             flops=flops, bytes_accessed=4 * volume.size + 4 * first_filter.size, transcendentals=0

time: 48.7 us -> 36.7 us (0.75)
  the two profiles are of different devices: /device:TPU:19 before, /device:TPU:1 now
where the time goes in v2:
time: 36.7 us; the launch traced here: 36.4 us
  Pallas kernels  34.5 us (94%)
  local copies, waits for them, and re-layouts  1.89 us (5%)
    pallas_call x1, Pallas kernels, per_device(): pl.pallas_call(functools.partial(kernel, n_space), out_shape=jax.ShapeDty...  34.5 us
    unnamed x1, local copies, waits for them, and re-layouts  1.89 us

profile of v2, /device:TPU:1, one launch (start us, length us, event | category | flops | bytes accessed | tf_op | source)
XLA Modules:
  0.0 36.4 jit_solution(14807061237182436671)
XLA Ops:
  0.0 34.5 %shard_map.37 = bf16[8,2,128,128]{3,2,1,0:T(8,128)(2,1)} custom-call(bf16[8,2,128,128]{3,2,1,0:T(8,128)(2,1)} %volume.1, bf16[3,3,3,256,128]{4,3,2,1,0:T(8,128)(2,1)} %first.1, bf16[3,3,3,256,128]{4,3,2,1,0:T(8,128)(2,1)} %second.1), custom_call_target="tpu_custom_call" | custom-call | flops 7247757312 | bytes 4587520 | tf_op jit(solution)/shard_map/pallas_call | solution.py:223
  34.5 1.9 %copy.5 = bf16[8,2,128,128]{3,2,1,0:T(8,128)(2,1)} copy(bf16[8,2,128,128]{3,2,1,0:T(8,128)(2,1)} %shard_map.37) | data formatting | bytes 1048576

commit v3 on v2

--- a/solution.py
+++ b/solution.py
@@ -220,9 +220,12 @@
     plane_buf = pltpu.VMEM((2, depth + 2, planes + 2, width, half), jnp.bfloat16)
     filter_buf = pltpu.VMEM((taps_d, taps_h, in_c, taps_w * out_c), jnp.bfloat16)
     flops = 2 * 2 * 27 * depth * planes * width * in_c * out_c
+    volume, first_filter, second_filter = (
+        pltpu.with_memory_space_constraint(x, pltpu.HBM) for x in (volume, first_filter, second_filter)
+    )
     return pl.pallas_call(
         functools.partial(kernel, n_space),
-        out_shape=jax.ShapeDtypeStruct(volume.shape, jnp.bfloat16),
+        out_shape=pltpu.VMEM(volume.shape, jnp.bfloat16),
         in_specs=[pl.BlockSpec(memory_space=pltpu.HBM)] * 3,
         out_specs=pl.BlockSpec(memory_space=pltpu.VMEM),
         scratch_shapes=[
@@ -235,7 +238,7 @@
             pltpu.SemaphoreType.DMA((2, 5, depth)),
         ],
         compiler_params=pltpu.CompilerParams(
-            collective_id=0, has_side_effects=True, vmem_limit_bytes=60 << 20
+            collective_id=0, has_side_effects=True, vmem_limit_bytes=32 << 20
         ),
         cost_estimate=pl.CostEstimate(
             flops=flops, bytes_accessed=4 * volume.size + 4 * first_filter.size, transcendentals=0

time: 36.7 us -> 34.8 us (0.948)
  local copies, waits for them, and re-layouts: 1.89 us -> 0.8 us
  Pallas kernels: 34.5 us -> 33.7 us
    unnamed x1, local copies, waits for them, and re-layouts: 1.89 us -> 0.8 us
    pallas_call x1, Pallas kernels: 34.5 us -> 33.7 us  [per_device(): pl.pallas_call(functools.partial(kernel, n_space), out_shape=pltpu.VMEM(v...]
where the time goes in v3:
time: 34.8 us; the launch traced here: 34.5 us
  Pallas kernels  33.7 us (97%)
  local copies, waits for them, and re-layouts  0.8 us (2%)
    pallas_call x1, Pallas kernels, per_device(): pl.pallas_call(functools.partial(kernel, n_space), out_shape=pltpu.VMEM(v...  33.7 us
    unnamed x1, local copies, waits for them, and re-layouts  0.8 us

profile of v3, /device:TPU:1, one launch (start us, length us, event | category | flops | bytes accessed | tf_op | source)
XLA Modules:
  0.0 34.5 jit_solution(10955060184981327744)
XLA Ops:
  0.0 33.7 %shard_map.37 = bf16[8,2,128,128]{3,2,1,0:T(8,128)(2,1)S(1)} custom-call(bf16[8,2,128,128]{3,2,1,0:T(8,128)(2,1)} %volume.1, bf16[3,3,3,256,128]{4,3,2,1,0:T(8,128)(2,1)} %first.1, bf16[3,3,3,256,128]{4,3,2,1,0:T(8,128)(2,1)} %second.1), custom_call_target="tpu_custom_call" | custom-call | flops 7247757312 | bytes 4587520 | tf_op jit(solution)/shard_map/pallas_call | solution.py:226
  33.7 0.8 %copy.5 = bf16[8,2,128,128]{3,2,1,0:T(8,128)(2,1)} copy(bf16[8,2,128,128]{3,2,1,0:T(8,128)(2,1)S(1)} %shard_map.37) | data formatting | bytes 1048576

commit v4 on v3

--- a/solution.py
+++ b/solution.py
@@ -8,7 +8,7 @@
 from jax.sharding import PartitionSpec as P
 
 MESH = pl.DeviceIdType.MESH
-LEADS = (4, 4)
+LEADS = (4, 5)
 CHAN, OWN_UP, OWN_DOWN, FWD_UP, FWD_DOWN = range(5)
 
 
@@ -24,7 +24,7 @@
 
 def kernel(
     n_space, volume, first, second, out,
-    field, hidden, w1, w2, local_sem, send_sem, recv_sem,
+    field, hidden, partials, w1, w2, local_sem, send_sem, recv_sem,
 ):
     s, c = lax.axis_index("space"), lax.axis_index("chan")
     other = 1 - c
@@ -140,18 +140,27 @@
             remote(phase, OWN_DOWN, d).wait_recv()
             remote(phase, FWD_DOWN, d).wait_recv()
 
-    def conv(buf, w, d):
-        pieces = [
-            buf[h, d + a, b : b + planes].reshape(planes * width, half)
-            for a in range(3)
-            for b in range(3)
-            for h in range(2)
-        ]
-        lhs = jnp.concatenate(pieces, axis=1)
-        partial = jnp.dot(
-            lhs, w[...].reshape(lhs.shape[1], 3 * out_c), preferred_element_type=jnp.float32
+    def dot_planes(buf, w, d, plane, taps):
+        lhs = jnp.concatenate(
+            [buf[h, d + a, plane + b] for a in range(3) for b in taps for h in range(2)], axis=1
         )
-        return [shifted_out(partial[p * width : (p + 1) * width], out_c) for p in range(planes)]
+        rows = w[:, taps[0] : taps[-1] + 1].reshape(lhs.shape[1], 3 * out_c)
+        return jnp.dot(lhs, rows, preferred_element_type=jnp.float32)
+
+    def inner_part(buf, w, d):
+        for p in range(planes):
+            taps = [b for b in range(3) if 1 <= p + b <= planes]
+            partials[d, p] = dot_planes(buf, w, d, p, taps)
+
+    def outer_part(buf, w, d):
+        totals = []
+        for p in range(planes):
+            total = partials[d, p]
+            for b in range(3):
+                if not 1 <= p + b <= planes:
+                    total = total + dot_planes(buf, w, d, p, [b])
+            totals.append(shifted_out(total, out_c))
+        return totals
 
     def send_volume(d, carry):
         send_own(0, d)
@@ -163,11 +172,17 @@
         copy.wait()
 
     def conv_phase(phase, lead, finish):
+        buf, w = (field, w1) if phase == 0 else (hidden, w2)
+
         def step(t, carry):
             @pl.when(t < depth)
             def _():
                 forward(phase, t)
 
+            @pl.when(jnp.logical_and(t >= 1, t <= depth))
+            def _():
+                inner_part(buf, w, t - 1)
+
             @pl.when(jnp.logical_and(t >= lead - 1, t < lead - 1 + depth))
             def _():
                 await_halo(phase, t - (lead - 1))
@@ -181,12 +196,12 @@
         lax.fori_loop(0, depth + lead, step, 0)
 
     def finish_hidden(d):
-        for p, total in enumerate(conv(field, w1, d)):
+        for p, total in enumerate(outer_part(field, w1, d)):
             hidden[c, d + 1, p + 1] = jnp.maximum(total, 0.0).astype(hidden.dtype)
         send_own(1, d)
 
     def finish_out(d):
-        for p, total in enumerate(conv(hidden, w2, d)):
+        for p, total in enumerate(outer_part(hidden, w2, d)):
             total = total + field[c, d + 1, p + 1].astype(jnp.float32)
             out[d, p] = jnp.maximum(total, 0.0).astype(out.dtype)
 
@@ -231,6 +246,7 @@
         scratch_shapes=[
             plane_buf,
             plane_buf,
+            pltpu.VMEM((depth, planes, width, taps_w * out_c), jnp.float32),
             filter_buf,
             filter_buf,
             pltpu.SemaphoreType.DMA((7,)),

time: 34.8 us -> 33.6 us (0.966)
  Pallas kernels: 33.7 us -> 32.6 us
    pallas_call x1, Pallas kernels: 33.7 us -> 32.6 us  [per_device(): pl.pallas_call(functools.partial(kernel, n_space), out_shape=pltpu.VMEM(v...]
where the time goes in v4:
time: 33.6 us; the launch traced here: 33.4 us
  Pallas kernels  32.6 us (97%)
  local copies, waits for them, and re-layouts  0.8 us (2%)
    pallas_call x1, Pallas kernels, per_device(): pl.pallas_call(functools.partial(kernel, n_space), out_shape=pltpu.VMEM(v...  32.6 us
    unnamed x1, local copies, waits for them, and re-layouts  0.8 us

profile of v4, /device:TPU:1, one launch (start us, length us, event | category | flops | bytes accessed | tf_op | source)
XLA Modules:
  0.0 33.4 jit_solution(15002739498226596934)
XLA Ops:
  0.0 32.6 %shard_map.37 = bf16[8,2,128,128]{3,2,1,0:T(8,128)(2,1)S(1)} custom-call(bf16[8,2,128,128]{3,2,1,0:T(8,128)(2,1)} %volume.1, bf16[3,3,3,256,128]{4,3,2,1,0:T(8,128)(2,1)} %first.1, bf16[3,3,3,256,128]{4,3,2,1,0:T(8,128)(2,1)} %second.1), custom_call_target="tpu_custom_call" | custom-call | flops 7247757312 | bytes 4587520 | tf_op jit(solution)/shard_map/pallas_call | solution.py:241
  32.6 0.8 %copy.5 = bf16[8,2,128,128]{3,2,1,0:T(8,128)(2,1)} copy(bf16[8,2,128,128]{3,2,1,0:T(8,128)(2,1)S(1)} %shard_map.37) | data formatting | bytes 1048576

commit v5 on v4

--- a/solution.py
+++ b/solution.py
@@ -32,23 +32,6 @@
     out_c = first.shape[4]
     has_up, has_down = s < n_space - 1, s > 0
     up, down, across = {"space": s + 1}, {"space": s - 1}, {"chan": other}
-
-    own_copy = pltpu.make_async_copy(
-        volume, field.at[c, pl.ds(1, depth), pl.ds(1, planes)], local_sem.at[0]
-    )
-    own_copy.start()
-    filter_copies = []
-    for k, (src, dst) in enumerate(((first, w1), (second, w2))):
-        for tap in range(3):
-            filter_copies.append(
-                pltpu.make_async_copy(
-                    src.at[:, :, tap],
-                    dst.at[:, :, :, pl.ds(tap * out_c, out_c)],
-                    local_sem.at[1 + 3 * k + tap],
-                )
-            )
-    for copy in filter_copies:
-        copy.start()
 
     barrier = pltpu.get_barrier_semaphore()
     pl.semaphore_signal(barrier, inc=1, device_id=across, device_id_type=MESH)
@@ -167,6 +150,24 @@
         return carry
 
     lax.fori_loop(0, depth, send_volume, 0)
+
+    own_copy = pltpu.make_async_copy(
+        volume, field.at[c, pl.ds(1, depth), pl.ds(1, planes)], local_sem.at[0]
+    )
+    own_copy.start()
+    filter_copies = []
+    for k, (src, dst) in enumerate(((first, w1), (second, w2))):
+        for tap in range(3):
+            filter_copies.append(
+                pltpu.make_async_copy(
+                    src.at[:, :, tap],
+                    dst.at[:, :, :, pl.ds(tap * out_c, out_c)],
+                    local_sem.at[1 + 3 * k + tap],
+                )
+            )
+    for copy in filter_copies:
+        copy.start()
+
     own_copy.wait()
     for copy in filter_copies[:3]:
         copy.wait()

time: 33.6 us -> 33.6 us (level)
  no operation moved by 1% of the time
where the time goes in v5:
time: 33.6 us; the launch traced here: 33.4 us
  Pallas kernels  32.6 us (97%)
  local copies, waits for them, and re-layouts  0.8 us (2%)
    pallas_call x1, Pallas kernels, per_device(): pl.pallas_call(functools.partial(kernel, n_space), out_shape=pltpu.VMEM(v...  32.6 us
    unnamed x1, local copies, waits for them, and re-layouts  0.8 us

profile of v5, /device:TPU:1, one launch (start us, length us, event | category | flops | bytes accessed | tf_op | source)
XLA Modules:
  0.0 33.4 jit_solution(3797556734745349235)
XLA Ops:
  0.0 32.6 %shard_map.37 = bf16[8,2,128,128]{3,2,1,0:T(8,128)(2,1)S(1)} custom-call(bf16[8,2,128,128]{3,2,1,0:T(8,128)(2,1)} %volume.1, bf16[3,3,3,256,128]{4,3,2,1,0:T(8,128)(2,1)} %first.1, bf16[3,3,3,256,128]{4,3,2,1,0:T(8,128)(2,1)} %second.1), custom_call_target="tpu_custom_call" | custom-call | flops 7247757312 | bytes 4587520 | tf_op jit(solution)/shard_map/pallas_call | solution.py:242
  32.6 0.8 %copy.5 = bf16[8,2,128,128]{3,2,1,0:T(8,128)(2,1)} copy(bf16[8,2,128,128]{3,2,1,0:T(8,128)(2,1)S(1)} %shard_map.37) | data formatting | bytes 1048576

commit v6 on v4

--- a/solution.py
+++ b/solution.py
@@ -108,15 +108,15 @@
         )
 
     def send_own(phase, d):
+        @pl.when(has_up)
+        def _():
+            remote(phase, OWN_UP, d).start()
+
+        @pl.when(has_down)
+        def _():
+            remote(phase, OWN_DOWN, d).start()
+
         remote(phase, CHAN, d).start()
-
-        @pl.when(has_up)
-        def _():
-            remote(phase, OWN_UP, d).start()
-
-        @pl.when(has_down)
-        def _():
-            remote(phase, OWN_DOWN, d).start()
 
     def forward(phase, d):
         remote(phase, CHAN, d).wait_recv()

time: 33.6 us -> 33.6 us (level)
  no operation moved by 1% of the time
where the time goes in v6:
time: 33.6 us; the launch traced here: 33.5 us
  Pallas kernels  32.7 us (97%)
  local copies, waits for them, and re-layouts  0.8 us (2%)
    pallas_call x1, Pallas kernels, per_device(): pl.pallas_call(functools.partial(kernel, n_space), out_shape=pltpu.VMEM(v...  32.7 us
    unnamed x1, local copies, waits for them, and re-layouts  0.8 us

profile of v6, /device:TPU:1, one launch (start us, length us, event | category | flops | bytes accessed | tf_op | source)
XLA Modules:
  0.0 33.5 jit_solution(13957510040892718371)
XLA Ops:
  0.0 32.7 %shard_map.37 = bf16[8,2,128,128]{3,2,1,0:T(8,128)(2,1)S(1)} custom-call(bf16[8,2,128,128]{3,2,1,0:T(8,128)(2,1)} %volume.1, bf16[3,3,3,256,128]{4,3,2,1,0:T(8,128)(2,1)} %first.1, bf16[3,3,3,256,128]{4,3,2,1,0:T(8,128)(2,1)} %second.1), custom_call_target="tpu_custom_call" | custom-call | flops 7247757312 | bytes 4587520 | tf_op jit(solution)/shard_map/pallas_call | solution.py:241
  32.7 0.8 %copy.5 = bf16[8,2,128,128]{3,2,1,0:T(8,128)(2,1)} copy(bf16[8,2,128,128]{3,2,1,0:T(8,128)(2,1)S(1)} %shard_map.37) | data formatting | bytes 1048576
